TPU v7x, 32 devices: a whole 2x2x4 slice. The times are simulated.
32 devices in a mesh: grp: 8 (over y, x, core), tp: 4 (over z).
Axes of the slice: x: 2, y: 2, z: 4, core: 2. Of those that a mesh axis runs over, the one named last changes fastest.
Arguments:
- text_embeds: bfloat16 [16384, 8192], P('grp', 'tp'), may hold values from -6 to 6
- image_embeds: bfloat16 [8192, 8192], P(('grp', 'tp')), may hold values from -6 to 6
- image_offsets: int32 [16, 2], P('grp'), may hold values from 0 to 768, as said below
- image_counts: int32 [16], P('grp'), may hold values from 1 to 2
- seq_lengths: int32 [16], P('grp'), may hold values from 513 to 1024
- norm_gain: bfloat16 [8192], P('tp'), may hold values from 0.25 to 1.75
- key_weight: bfloat16 [8192, 512], P('tp'), may hold values from -0.0625 to 0.0625
- key_bias: bfloat16 [512], replicated, may hold values from -3 to 3
- key_cotangent: bfloat16 [16384, 512], P(('grp', 'tp')), may hold values from -0.017944336 to 0.017944336
Outputs:
- key_states: bfloat16 [16384, 512], P(('grp', 'tp'))
- weight_grad: float32 [8192, 512], P('tp')
- bias_grad: float32 [512], replicated
- gain_grad: float32 [8192], P('tp')
Inputs may be any that keep to these rules, and one draw needn't show every extreme that they name: `image_offsets`: each sequence's first image_counts slots hold increasing starts of non-intersecting runs of 256 rows that end within its used rows; later slots hold 0.
All inputs are finite; a program needn't handle non-finite values.
Results may differ from a plain program's by a relative error of at most 0.0046.
Values may be sent and summed in bfloat16 or wider, within the bound.
A program may use at most 64 MiB of HBM per device.

v0:
```python
import jax
import jax.numpy as jnp
from jax import lax
from jax.sharding import PartitionSpec as P

EPS = 1e-06
F32 = jnp.float32
BF16 = jnp.bfloat16


def on_device(
    text_embeds,
    image_embeds,
    image_offsets,
    image_counts,
    seq_lengths,
    norm_gain,
    key_weight,
    key_bias,
    key_cotangent,
):
    n_tp = lax.axis_size("tp")
    me = lax.axis_index("tp")
    rows = text_embeds.shape[0]
    width = image_embeds.shape[1]
    seqs, slots = image_offsets.shape
    length = rows // seqs
    own_image = image_embeds.shape[0]
    image_total = own_image * n_tp
    patch = image_total // (seqs * slots)
    own_count = key_cotangent.shape[0]
    image_rows = lax.all_to_all(image_embeds, "tp", split_axis=1, concat_axis=0, tiled=True)
    position = lax.broadcasted_iota(jnp.int32, (seqs, length), 1)
    row_valid = (position < seq_lengths[:, None]).astype(F32).reshape(rows)
    own_valid = lax.dynamic_slice_in_dim(row_valid, me * own_count, own_count, 0)
    own_grad = lax.optimization_barrier(
        (key_cotangent.astype(F32) * own_valid[:, None]).astype(BF16)
    )
    masked_grad = lax.all_gather(own_grad, "tp", axis=0, tiled=True)
    bias_grad = lax.psum(jnp.sum(own_grad.astype(F32), axis=0), ("grp", "tp"))
    text32 = text_embeds.astype(F32)
    image32 = image_embeds.astype(F32)
    image_squares = lax.dynamic_update_slice_in_dim(
        jnp.zeros((image_total,), F32), jnp.sum(image32 * image32, axis=1), me * own_image, 0
    )
    squares = lax.psum(jnp.concatenate([jnp.sum(text32 * text32, axis=1), image_squares]), "tp")
    rstd = lax.rsqrt(squares / width + EPS)
    slot_used = lax.broadcasted_iota(jnp.int32, (seqs, slots), 1) < image_counts[:, None]
    inside = jnp.zeros((seqs, length), jnp.bool_)
    source = jnp.zeros((seqs, length), jnp.int32)
    first = lax.broadcasted_iota(jnp.int32, (seqs, length), 0) * (slots * patch)
    for k in range(slots):
        start = image_offsets[:, k : k + 1]
        here = slot_used[:, k : k + 1] & (position >= start) & (position < start + patch)
        source = jnp.where(here, first + k * patch + position - start, source)
        inside = inside | here
    text_rstd = rstd[:rows] * (1.0 - inside.astype(F32).reshape(rows))
    image_rstd = rstd[rows:]
    used = jnp.repeat(slot_used.reshape(-1).astype(F32), patch)
    gain32 = norm_gain.astype(F32)
    scaled_weight = (key_weight.astype(F32) * gain32[:, None]).astype(BF16)
    partial = (
        jnp.dot(text_embeds, scaled_weight, preferred_element_type=F32) * text_rstd[:, None]
    ).astype(BF16)
    text_grad = (masked_grad.astype(F32) * text_rstd[:, None]).astype(BF16)
    slot_starts = (
        lax.broadcasted_iota(jnp.int32, (seqs, slots), 0) * length + image_offsets
    ).reshape(-1)
    image_at = (
        slot_starts[:, None] + lax.broadcasted_iota(jnp.int32, (seqs * slots, patch), 1)
    ).reshape(-1)
    picked = jnp.take(masked_grad, image_at, axis=0, mode="clip")
    image_grad = (picked.astype(F32) * (image_rstd * used)[:, None]).astype(BF16)
    over_rows = (((0,), (0,)), ((), ()))
    text_part = lax.dot_general(text_embeds, text_grad, over_rows, preferred_element_type=F32)
    image_keys = (
        jnp.dot(image_rows, scaled_weight, preferred_element_type=F32) * image_rstd[:, None]
    ).astype(BF16)
    placed = jnp.take(image_keys, source.reshape(rows), axis=0, mode="clip")
    partial = jnp.where(inside.reshape(rows)[:, None], placed, partial)
    partial, masked_grad, bias_grad = lax.optimization_barrier((partial, masked_grad, bias_grad))
    projected = lax.psum_scatter(partial, "tp", scatter_dimension=0, tiled=True)
    key_states = (
        (projected.astype(F32) + key_bias.astype(F32)[None, :]) * own_valid[:, None]
    ).astype(BF16)
    image_part = lax.dot_general(image_rows, image_grad, over_rows, preferred_element_type=F32)
    total = lax.psum((text_part + image_part).astype(BF16), "grp").astype(F32)
    weight_grad = total * gain32[:, None]
    gain_grad = jnp.sum(total * key_weight.astype(F32), axis=1)
    return (key_states, weight_grad, bias_grad, gain_grad)


def solution(mesh):
    placed = (
        P("grp", "tp"),
        P(("grp", "tp"), None),
        P("grp", None),
        P("grp"),
        P("grp"),
        P("tp"),
        P("tp", None),
        P(),
        P(("grp", "tp"), None),
    )
    return jax.shard_map(
        on_device,
        mesh=mesh,
        in_specs=placed,
        out_specs=(P(("grp", "tp"), None), P("tp", None), P(), P("tp")),
        check_vma=False,
    )
```

profile of v0, /device:TPU:0, one launch (start us, length us, event | category | flops | bytes accessed | tf_op | source)
XLA Modules:
  0.0 348.3 jit_solution(14095932493099703073)
XLA Ops:
  7.2 6.4 %copy.28 = bf16[256,8192]{0,1:T(8,128)(2,1)} copy(bf16[256,8192]{1,0:T(8,128)(2,1)} %param.10) | data formatting | bytes 8388608 | tf_op args[1]
  13.6 6.6 %all-to-all-start = ((bf16[256,4,2048]{0,2,1:T(8,128)(2,1)}), bf16[256,4,2048]{0,2,1:T(8,128)(2,1)}, u32[]{:S(2)}, u32[]{:S(2)}) async-start(bf16[256,4,2048]{0,2,1:T(8,128)(2,1)} %bitcast.74), calls=%async_computation | async-start | bytes 8388608 | tf_op jit(solution)/shard_map/all_to_all | solution.py:32
  20.2 0.1 fusion.16
  20.3 0.2 copy.32
  20.5 0.1 dynamic_slice.3
  20.6 0.9 multiply_convert_fusion.7
  21.5 0.0 all-gather.2.cloned.1.call-update
  21.5 0.0 all-reduce.2.cloned.1.call-start
  21.5 0.1 fusion.17
  21.6 0.2 slice_reduce_fusion.1
  21.8 0.2 add_reduce_fusion.1
  22.0 0.1 and_or_fusion
  22.2 0.1 broadcast_bitcast_fusion.4
  22.3 0.1 broadcast_bitcast_fusion.6
  22.4 0.1 broadcast_bitcast_fusion.3
  22.5 0.1 broadcast_bitcast_fusion.2
  22.6 0.1 reshape.320
  22.7 0.1 broadcast_add_fusion
  22.7 0.1 broadcast_bitcast_fusion.8
  22.9 2.5 copy.27
  25.4 0.1 add.101
  25.5 0.1 add_bitcast_fusion
  25.6 3.1 multiply_reduce_fusion.1
  28.7 0.3 dynamic_update_slice.3
  28.9 0.1 convert_reduce_fusion
  29.1 138.5 %psum.22 = f32[512]{0:T(512)} all-reduce(f32[512]{0:T(512)S(1)} %convert_reduce_fusion), channel_id=1, replica_groups=mesh['grp'=8,'tp'=4] {'grp','tp'}, use_global_device_ids=true, to_apply=%region_4.0 | all-reduce | flops 512 | bytes 4096 | tf_op jit(solution)/shard_map/psum | solution.py:40
  167.6 5.1 %multiply_reduce_fusion = f32[2048]{0:T(1024)S(1)} fusion(bf16[2048,2048]{1,0:T(8,128)(2,1)} %param.9), kind=kLoop, calls=%fused_computation.2 | loop fusion | flops 12580864 | bytes 8396800 | tf_op jit(solution)/shard_map/reduce_sum | solution.py:46
  172.7 17.7 %psum.21 = f32[3072]{0:T(1024)S(1)} all-reduce(f32[3072]{0:T(1024)S(1)} %pad_maximum_fusion), channel_id=1, replica_groups=mesh['grp'=8,'tp'=4] {'tp'}, use_global_device_ids=true, to_apply=%region_2.0 | all-reduce | flops 3072 | bytes 24576 | tf_op jit(solution)/shard_map/psum | solution.py:46
  190.4 0.1 and_select_fusion.1
  190.5 0.0 all-gather.2.cloned.1.call-done
  190.5 2.9 copy.33
  193.4 5.1 %gather_fusion.1 = bf16[1024,512]{1,0:T(8,128)(2,1)} fusion(bf16[2048,512]{1,0:T(8,128)(2,1)S(1)} %copy.33, s32[1024]{0:T(1024)S(1)} %broadcast_clamp_fusion.1), kind=kCustom, calls=%fused_computation.1 | custom fusion | bytes 2101248 | tf_op jit(solution)/shard_map/jit(_take)/gather | solution.py:72
  198.5 6.3 %copy.29 = bf16[4,256,2048]{2,1,0:T(8,128)(2,1)} copy(bf16[4,256,2048]{1,2,0:T(8,128)(2,1)} %bitcast.1) | data formatting | bytes 8388608 | tf_op jit(solution)/shard_map/all_to_all | solution.py:32
  204.8 4.6 %fusion.11 = bf16[1024,512]{0,1:T(8,128)(2,1)S(1)} fusion(bf16[1024,2048]{1,0:T(8,128)(2,1)} %bitcast.72, bf16[2048,512]{0,1:T(8,128)(2,1)S(1)} %copy-done, f32[2048]{0:T(1024)S(1)} %convert_element_type.85, f32[1024]{0:T(1024)S(1)} %get-tuple-element.29), kind=kOutput, calls=%fused_computation.19 | convolution fusion | flops 2151677952 | bytes 7352320 | tf_op jit(solution)/shard_map/dot_general | solution.py:77
  209.4 0.5 copy.30
  209.9 7.5 %gather_fusion = bf16[2048,512]{1,0:T(8,128)(2,1)S(1)} fusion(bf16[1024,512]{1,0:T(8,128)(2,1)S(1)} %copy.30, s32[2048]{0:T(1024)S(1)} %broadcast_clamp_fusion), kind=kCustom, calls=%fused_computation | custom fusion | bytes 4202496 | tf_op jit(solution)/shard_map/jit(_take)/gather | solution.py:79
  217.5 2.5 copy.31
  220.0 4.9 %fusion.14 = f32[512,2048]{1,0:T(8,128)S(1)} fusion(bf16[1024,2048]{1,0:T(8,128)(2,1)} %bitcast.73, bf16[1024,512]{1,0:T(8,128)(2,1)S(1)} %copy-done.2, f32[1024]{0:T(1024)S(1)} %get-tuple-element.28), kind=kOutput, calls=%fused_computation.20 | convolution fusion | flops 2149056512 | bytes 9441280 | tf_op jit(solution)/shard_map/dot_general | solution.py:86
  224.9 9.3 %fusion.3 = bf16[2048,512]{0,1:T(8,128)(2,1)} fusion(f32[512,2048]{1,0:T(8,128)S(1)} %fusion.14, bf16[2048,2048]{1,0:T(8,128)(2,1)} %param.9, bf16[2048,512]{0,1:T(8,128)(2,1)S(1)} %copy-done.5, f32[2048]{0:T(1024)S(1)} %slice_multiply_fusion), kind=kOutput, calls=%fused_computation.13 | convolution fusion | flops 4300210176 | bytes 16785408 | tf_op jit(solution)/shard_map/dot_general | solution.py:75
  234.2 0.0 all-reduce.2.cloned.1.call-update
  234.3 0.3 reduce-scatter.2.cloned.1.call-start
  234.5 9.6 %fusion.4 = bf16[2048,512]{0,1:T(8,128)(2,1)} fusion(bf16[2048,512]{0,1:T(8,128)(2,1)} %copy.31, bf16[2048,2048]{1,0:T(8,128)(2,1)} %param.9, f32[2048]{0:T(1024)S(1)} %slice_multiply_fusion, pred[2048]{0:T(1024)(128)(4,1)S(1)} %or.12, bf16[2048,512]{0,1:T(8,128)(2,1)S(1)} %copy-done.1, f32[2048]{0:T(1024)S(1)} %convert_element_type.85), kind=kOutput, calls=%fused_computation.14 | convolution fusion | flops 4301258752 | bytes 14698496 | tf_op jit(solution)/shard_map/dot_general | solution.py:63
  244.2 50.3 %all-reduce.2.cloned.1.call-done = bf16[2048,512]{0,1:T(8,128)(2,1)} async-done(((bf16[2048,512]{0,1:T(8,128)(2,1)}), bf16[2048,512]{0,1:T(8,128)(2,1)}) %all-reduce.2.cloned.1.call-update) | async-done | bytes 2097168 | tf_op jit(solution)/shard_map/psum | solution.py:87
  294.4 4.9 %fusion.1 = (f32[2048]{0:T(1024)}, f32[2048,512]{0,1:T(8,128)}) fusion(bf16[2048,512]{0,1:T(8,128)(2,1)S(1)} %copy-done.1, bf16[2048,512]{0,1:T(8,128)(2,1)} %all-reduce.2.cloned.1.call-done, f32[2048]{0:T(1024)S(1)} %convert_element_type.85), kind=kLoop, calls=%fused_computation.8 | loop fusion | flops 5240832 | bytes 8404992 | tf_op jit(solution)/shard_map/reduce_sum | solution.py:89
  299.4 5.4 %copy.35 = f32[2048,512]{1,0:T(8,128)} copy(f32[2048,512]{0,1:T(8,128)} %get-tuple-element.27) | data formatting | bytes 8388608
  304.8 34.7 %reduce-scatter.2.cloned.1.call-done = bf16[512,512]{0,1:T(8,128)(2,1)} async-done(((bf16[2048,512]{0,1:T(8,128)(2,1)}), bf16[512,512]{0,1:T(8,128)(2,1)}) %reduce-scatter.2.cloned.1.call-update) | async-done | bytes 524304 | tf_op jit(solution)/shard_map/reduce_scatter | solution.py:82
  339.5 1.2 multiply_convert_fusion.6
  340.7 1.0 copy.34
  (53 shorter events, 0.3 us)
Async XLA Ops:
  13.5 6.7 %copy-start.10 = (s32[2]{0:T(128)S(1)}, s32[2]{0:T(128)}, u32[]{:S(2)}) copy-start(s32[2]{0:T(128)} %param.13) | copy-start | bytes 28
  13.5 6.7 %copy-start.6 = (bf16[512,512]{1,0:T(8,128)(2,1)S(1)}, bf16[512,512]{1,0:T(8,128)(2,1)}, u32[]{:S(2)}) copy-start(bf16[512,512]{1,0:T(8,128)(2,1)} %param.17) | copy-start | bytes 1572868
  13.5 8.0 %copy-start.11 = (s32[2]{0:T(128)S(1)}, s32[2]{0:T(128)}, u32[]{:S(2)}) copy-start(s32[2]{0:T(128)} %param.12) | copy-start | bytes 28
  13.5 8.3 %copy-start.7 = (s32[2,2]{1,0:T(2,128)S(1)}, s32[2,2]{1,0:T(2,128)}, u32[]{:S(2)}) copy-start(s32[2,2]{1,0:T(2,128)} %param.11) | copy-start | bytes 52
  13.5 9.3 %copy-start.4 = (bf16[2048,512]{1,0:T(8,128)(2,1)S(1)}, bf16[2048,512]{1,0:T(8,128)(2,1)}, u32[]{:S(2)}) copy-start(bf16[2048,512]{1,0:T(8,128)(2,1)} %param.15) | copy-start | bytes 6291460
  13.6 184.9 %all-to-all-start = ((bf16[256,4,2048]{0,2,1:T(8,128)(2,1)}), bf16[256,4,2048]{0,2,1:T(8,128)(2,1)}, u32[]{:S(2)}, u32[]{:S(2)}) async-start(bf16[256,4,2048]{0,2,1:T(8,128)(2,1)} %bitcast.74), calls=%async_computation | async-start | bytes 8388608 | tf_op jit(solution)/shard_map/all_to_all | solution.py:32
  20.2 5.2 %copy-start.8 = (bf16[2048]{0:T(1024)(128)(2,1)S(1)}, bf16[2048]{0:T(1024)(128)(2,1)}, u32[]{:S(2)}) copy-start(bf16[2048]{0:T(1024)(128)(2,1)} %param.14) | copy-start | bytes 12292
  20.2 170.3 %all-gather.2.cloned.1.call-start = ((), (), s32[]{:S(2)}) async-start(), calls=%async_computation.2 | async-start | bytes 2621440 | tf_op jit(solution)/shard_map/all_gather | solution.py:39
  21.5 273.0 %all-reduce.2.cloned.1.call-start = ((), (), s32[]{:S(2)}) async-start(), calls=%async_computation.4 | async-start | bytes 4194304 | tf_op jit(solution)/shard_map/psum | solution.py:87
  22.8 6.1 %copy-start.3 = (bf16[512,512]{0,1:T(8,128)(2,1)S(1)}, bf16[512,512]{0,1:T(8,128)(2,1)}, u32[]{:S(2)}) copy-start(bf16[512,512]{0,1:T(8,128)(2,1)} %multiply_convert_fusion.7) | copy-start | bytes 1572868
  198.4 6.4 %copy-start = (bf16[2048,512]{0,1:T(8,128)(2,1)S(1)}, bf16[2048,512]{0,1:T(8,128)(2,1)}, u32[]{:S(2)}) copy-start(bf16[2048,512]{0,1:T(8,128)(2,1)} %copy.27) | copy-start | bytes 6291460
  217.5 2.5 copy-start.2
  220.0 4.9 %copy-start.5 = (bf16[2048,512]{0,1:T(8,128)(2,1)S(1)}, bf16[2048,512]{0,1:T(8,128)(2,1)}, u32[]{:S(2)}) copy-start(bf16[2048,512]{0,1:T(8,128)(2,1)} %all-gather.2.cloned.1.call-done) | copy-start | bytes 6291460
  224.9 9.6 %copy-start.1 = (bf16[2048,512]{0,1:T(8,128)(2,1)S(1)}, bf16[2048,512]{0,1:T(8,128)(2,1)}, u32[]{:S(2)}) copy-start(bf16[2048,512]{0,1:T(8,128)(2,1)} %copy.27) | copy-start | bytes 6291460
  234.3 9.9 %copy-start.9 = (bf16[512]{0:T(512)(128)(2,1)S(1)}, bf16[512]{0:T(512)(128)(2,1)}, u32[]{:S(2)}) copy-start(bf16[512]{0:T(512)(128)(2,1)} %param.16) | copy-start | bytes 3076
  234.3 105.2 %reduce-scatter.2.cloned.1.call-start = ((), (), s32[]{:S(2)}) async-start(), calls=%async_computation.3 | async-start | bytes 2621440 | tf_op jit(solution)/shard_map/reduce_scatter | solution.py:82
Sparse Core Ops, SparseCore 0:
  23.1 77.2 all-gather.1
  234.4 60.0 all-reduce.1
  296.7 42.6 reduce-scatter.1
where the time goes:
time: 349 us; the launch traced here: 348 us
  blocking collectives  156 us (45%)
  waiting for transfers between devices  85.1 us (24%)
  local copies, waits for them, and re-layouts  41.6 us (12%)
  matrix products  28.3 us (8%)
  other arithmetic  16.1 us (5%)
  between operations  14 us (4%)
  starting transfers between devices  6.93 us (2%)
    psum x1, blocking collectives, on_device(): bias_grad = lax.psum(jnp.sum(own_grad.astype(F32), axis=0), ('grp', 'tp'))  139 us
    psum x1, waiting for transfers between devices, on_device(): total = lax.psum((text_part + image_part).astype(BF16), 'grp').astype(F32)  50.3 us
    reduce_scatter x1, waiting for transfers between devices, on_device(): projected = lax.psum_scatter(partial, 'tp', scatter_dimension=0, tiled=True)  34.7 us
    psum x1, blocking collectives, on_device(): lax.psum(jnp.concatenate([jnp.sum(text32 * text32, axis=1), image_squares...  17.7 us
    unnamed x47, local copies, waits for them, and re-layouts  16 us
    gather x2, local copies, waits for them, and re-layouts, on_device(): placed = jnp.take(image_keys, source.reshape(rows), axis=0, mode='clip')  10 us
    dot_general x1, matrix products, on_device(): jnp.dot(text_embeds, scaled_weight, preferred_element_type=F32)  9.57 us
    dot_general x1, matrix products, on_device(): lax.dot_general(text_embeds, text_grad, over_rows, preferred_element_type...  9.33 us
  transfers between devices with their start and end apart: 4, of which 2 were waited for; matrix products, arithmetic and copies ran while one was open for 12% of the time, Pallas kernels for 0%

commit v1 on v0

--- a/solution.py
+++ b/solution.py
@@ -37,7 +37,9 @@
         (key_cotangent.astype(F32) * own_valid[:, None]).astype(BF16)
     )
     masked_grad = lax.all_gather(own_grad, "tp", axis=0, tiled=True)
-    bias_grad = lax.psum(jnp.sum(own_grad.astype(F32), axis=0), ("grp", "tp"))
+    bias_grad = jnp.sum(
+        lax.all_gather(jnp.sum(own_grad.astype(F32), axis=0), ("grp", "tp")), axis=0
+    )
     text32 = text_embeds.astype(F32)
     image32 = image_embeds.astype(F32)
     image_squares = lax.dynamic_update_slice_in_dim(

time: 349 us -> 387 us (1.11)
  blocking collectives: 156 us -> 195 us
    all_gather x0 -> x1, blocking collectives: none -> 179 us  [on_device(): lax.all_gather(jnp.sum(own_grad.astype(F32), axis=0), ('grp', 'tp'))]
    psum x1 -> x0, blocking collectives: 139 us -> none  [on_device(): bias_grad = lax.psum(jnp.sum(own_grad.astype(F32), axis=0), ('grp', 'tp'))]
  transfers between devices with their start and end apart: 4 -> 4, of which waited for: 2 -> 2; matrix products, arithmetic and copies ran while one was open for 12% -> 11% of each run, Pallas kernels for 0% -> 0%
where the time goes in v1:
time: 387 us
  blocking collectives  195 us (50%)
  waiting for transfers between devices  84 us (22%)
  local copies, waits for them, and re-layouts  41.6 us (11%)
  matrix products  28.6 us (7%)
  other arithmetic  16.7 us (4%)
  between operations  14 us (4%)
  starting transfers between devices  6.93 us (2%)
    all_gather x1, blocking collectives, on_device(): lax.all_gather(jnp.sum(own_grad.astype(F32), axis=0), ('grp', 'tp'))  179 us
    psum x1, waiting for transfers between devices, on_device(): total = lax.psum((text_part + image_part).astype(BF16), 'grp').astype(F32)  49.2 us
    reduce_scatter x1, waiting for transfers between devices, on_device(): projected = lax.psum_scatter(partial, 'tp', scatter_dimension=0, tiled=True)  34.7 us
    unnamed x47, local copies, waits for them, and re-layouts  16 us
    psum x1, blocking collectives, on_device(): lax.psum(jnp.concatenate([jnp.sum(text32 * text32, axis=1), image_squares...  15.7 us
    gather x2, local copies, waits for them, and re-layouts, on_device(): placed = jnp.take(image_keys, source.reshape(rows), axis=0, mode='clip')  10 us
    dot_general x1, matrix products, on_device(): jnp.dot(text_embeds, scaled_weight, preferred_element_type=F32)  9.85 us
    dot_general x1, matrix products, on_device(): lax.dot_general(text_embeds, text_grad, over_rows, preferred_element_type...  9.33 us
  transfers between devices with their start and end apart: 4, of which 2 were waited for; matrix products, arithmetic and copies ran while one was open for 11% of the time, Pallas kernels for 0%

profile of v1, /device:TPU:0, one launch (start us, length us, event | category | flops | bytes accessed | tf_op | source)
XLA Modules:
  0.0 386.6 jit_solution(9884755786478775773)
XLA Ops:
  7.2 6.4 %copy.37 = bf16[256,8192]{0,1:T(8,128)(2,1)} copy(bf16[256,8192]{1,0:T(8,128)(2,1)} %param.10) | data formatting | bytes 8388608 | tf_op args[1]
  13.6 6.6 %all-to-all-start = ((bf16[256,4,2048]{0,2,1:T(8,128)(2,1)}), bf16[256,4,2048]{0,2,1:T(8,128)(2,1)}, u32[]{:S(2)}, u32[]{:S(2)}) async-start(bf16[256,4,2048]{0,2,1:T(8,128)(2,1)} %bitcast.75), calls=%async_computation | async-start | bytes 8388608 | tf_op jit(solution)/shard_map/all_to_all | solution.py:32
  20.2 0.1 fusion.16
  20.3 0.2 copy.41
  20.5 0.1 dynamic_slice.3
  20.6 0.9 multiply_convert_fusion.7
  21.5 0.0 all-gather.4.cloned.1.call-update
  21.5 0.0 all-reduce.2.cloned.1.call-start
  21.5 0.1 fusion.17
  21.6 0.2 slice_reduce_fusion.1
  21.8 0.2 add_reduce_fusion.1
  22.0 0.1 and_or_fusion
  22.2 0.1 broadcast_bitcast_fusion.4
  22.3 0.1 broadcast_bitcast_fusion.6
  22.4 0.1 broadcast_bitcast_fusion.3
  22.5 0.1 broadcast_bitcast_fusion.2
  22.6 0.1 reshape.320
  22.7 0.1 broadcast_add_fusion
  22.7 0.1 broadcast_bitcast_fusion.8
  22.8 2.5 copy.36
  25.4 0.1 add.99
  25.5 0.1 add_bitcast_fusion
  25.6 0.2 convert_reduce_fusion
  25.7 179.0 %all-gather.1 = f32[32,1,512]{2,1,0:T(1,128)S(1)} all-gather(f32[1,1,512]{2,1,0:T(1,128)S(1)} %bitcast.89), channel_id=2, replica_groups=mesh['grp'=8,'tp'=4] {'grp','tp'}, dimensions={0}, use_global_device_ids=true | all-gather | bytes 67584 | tf_op jit(solution)/shard_map/all_gather | solution.py:41
  204.7 0.6 reduce_sum.48
  205.4 3.1 multiply_reduce_fusion.1
  208.5 0.3 dynamic_update_slice.3
  208.8 5.1 %multiply_reduce_fusion = f32[2048]{0:T(1024)S(1)} fusion(bf16[2048,2048]{1,0:T(8,128)(2,1)} %param.9), kind=kLoop, calls=%fused_computation.2 | loop fusion | flops 12580864 | bytes 8396800 | tf_op jit(solution)/shard_map/reduce_sum | solution.py:48
  213.8 15.7 %psum.14 = f32[3072]{0:T(1024)S(1)} all-reduce(f32[3072]{0:T(1024)S(1)} %pad_maximum_fusion), channel_id=1, replica_groups=mesh['grp'=8,'tp'=4] {'tp'}, use_global_device_ids=true, to_apply=%region_2.0 | all-reduce | flops 3072 | bytes 24576 | tf_op jit(solution)/shard_map/psum | solution.py:48
  229.6 0.1 and_select_fusion.1
  229.7 0.0 all-gather.4.cloned.1.call-done
  229.7 2.9 copy.42
  232.6 5.1 %gather_fusion.1 = bf16[1024,512]{1,0:T(8,128)(2,1)} fusion(bf16[2048,512]{1,0:T(8,128)(2,1)S(1)} %copy.42, s32[1024]{0:T(1024)S(1)} %broadcast_clamp_fusion.1), kind=kCustom, calls=%fused_computation.1 | custom fusion | bytes 2101248 | tf_op jit(solution)/shard_map/jit(_take)/gather | solution.py:74
  237.6 6.3 %copy.38 = bf16[4,256,2048]{2,1,0:T(8,128)(2,1)} copy(bf16[4,256,2048]{1,2,0:T(8,128)(2,1)} %bitcast.1) | data formatting | bytes 8388608 | tf_op jit(solution)/shard_map/all_to_all | solution.py:32
  244.0 4.6 %fusion.11 = bf16[1024,512]{0,1:T(8,128)(2,1)S(1)} fusion(bf16[1024,2048]{1,0:T(8,128)(2,1)} %bitcast.73, bf16[2048,512]{0,1:T(8,128)(2,1)S(1)} %copy-done, f32[2048]{0:T(1024)S(1)} %convert_element_type.85, f32[1024]{0:T(1024)S(1)} %get-tuple-element.33), kind=kOutput, calls=%fused_computation.19 | convolution fusion | flops 2151677952 | bytes 7352320 | tf_op jit(solution)/shard_map/dot_general | solution.py:79
  248.6 0.5 copy.39
  249.1 7.5 %gather_fusion = bf16[2048,512]{1,0:T(8,128)(2,1)S(1)} fusion(bf16[1024,512]{1,0:T(8,128)(2,1)S(1)} %copy.39, s32[2048]{0:T(1024)S(1)} %broadcast_clamp_fusion), kind=kCustom, calls=%fused_computation | custom fusion | bytes 4202496 | tf_op jit(solution)/shard_map/jit(_take)/gather | solution.py:81
  256.7 2.5 copy.40
  259.2 4.9 %fusion.14 = f32[512,2048]{1,0:T(8,128)S(1)} fusion(bf16[1024,2048]{1,0:T(8,128)(2,1)} %bitcast.74, bf16[1024,512]{1,0:T(8,128)(2,1)S(1)} %copy-done.2, f32[1024]{0:T(1024)S(1)} %get-tuple-element.32), kind=kOutput, calls=%fused_computation.20 | convolution fusion | flops 2149056512 | bytes 9441280 | tf_op jit(solution)/shard_map/dot_general | solution.py:88
  264.1 9.3 %fusion.3 = bf16[2048,512]{0,1:T(8,128)(2,1)} fusion(f32[512,2048]{1,0:T(8,128)S(1)} %fusion.14, bf16[2048,2048]{1,0:T(8,128)(2,1)} %param.9, bf16[2048,512]{0,1:T(8,128)(2,1)S(1)} %copy-done.5, f32[2048]{0:T(1024)S(1)} %slice_multiply_fusion), kind=kOutput, calls=%fused_computation.13 | convolution fusion | flops 4300210176 | bytes 16785408 | tf_op jit(solution)/shard_map/dot_general | solution.py:77
  273.4 0.3 reduce-scatter.2.cloned.1.call-start
  273.7 9.9 %fusion.4 = bf16[2048,512]{0,1:T(8,128)(2,1)} fusion(bf16[2048,512]{0,1:T(8,128)(2,1)} %copy.40, bf16[2048,2048]{1,0:T(8,128)(2,1)} %param.9, f32[2048]{0:T(1024)S(1)} %slice_multiply_fusion, pred[2048]{0:T(1024)(128)(4,1)S(1)} %or.12, bf16[2048,512]{0,1:T(8,128)(2,1)S(1)} %copy-done.1, f32[2048]{0:T(1024)S(1)} %convert_element_type.85), kind=kOutput, calls=%fused_computation.14 | convolution fusion | flops 4301258752 | bytes 14698496 | tf_op jit(solution)/shard_map/dot_general | solution.py:65
  283.6 49.2 %all-reduce.2.cloned.1.call-done = bf16[2048,512]{0,1:T(8,128)(2,1)} async-done(((bf16[2048,512]{0,1:T(8,128)(2,1)}), bf16[2048,512]{0,1:T(8,128)(2,1)}) %all-reduce.2.cloned.1.call-update) | async-done | bytes 2097168 | tf_op jit(solution)/shard_map/psum | solution.py:89
  332.8 4.9 %fusion.1 = (f32[2048]{0:T(1024)}, f32[2048,512]{0,1:T(8,128)}) fusion(bf16[2048,512]{0,1:T(8,128)(2,1)S(1)} %copy-done.1, bf16[2048,512]{0,1:T(8,128)(2,1)} %all-reduce.2.cloned.1.call-done, f32[2048]{0:T(1024)S(1)} %convert_element_type.85), kind=kLoop, calls=%fused_computation.8 | loop fusion | flops 5240832 | bytes 8404992 | tf_op jit(solution)/shard_map/reduce_sum | solution.py:91
  337.7 5.4 %copy.44 = f32[2048,512]{1,0:T(8,128)} copy(f32[2048,512]{0,1:T(8,128)} %get-tuple-element.31) | data formatting | bytes 8388608
  343.1 34.7 %reduce-scatter.2.cloned.1.call-done = bf16[512,512]{0,1:T(8,128)(2,1)} async-done(((bf16[2048,512]{0,1:T(8,128)(2,1)}), bf16[512,512]{0,1:T(8,128)(2,1)}) %reduce-scatter.2.cloned.1.call-update) | async-done | bytes 524304 | tf_op jit(solution)/shard_map/reduce_scatter | solution.py:84
  377.8 1.2 multiply_convert_fusion.6
  379.1 1.0 copy.43
  (54 shorter events, 0.3 us)
Async XLA Ops:
  13.5 6.7 %copy-start.10 = (s32[2]{0:T(128)S(1)}, s32[2]{0:T(128)}, u32[]{:S(2)}) copy-start(s32[2]{0:T(128)} %param.13) | copy-start | bytes 28
  13.5 6.7 %copy-start.6 = (bf16[512,512]{1,0:T(8,128)(2,1)S(1)}, bf16[512,512]{1,0:T(8,128)(2,1)}, u32[]{:S(2)}) copy-start(bf16[512,512]{1,0:T(8,128)(2,1)} %param.17) | copy-start | bytes 1572868
  13.5 8.0 %copy-start.11 = (s32[2]{0:T(128)S(1)}, s32[2]{0:T(128)}, u32[]{:S(2)}) copy-start(s32[2]{0:T(128)} %param.12) | copy-start | bytes 28
  13.5 8.3 %copy-start.7 = (s32[2,2]{1,0:T(2,128)S(1)}, s32[2,2]{1,0:T(2,128)}, u32[]{:S(2)}) copy-start(s32[2,2]{1,0:T(2,128)} %param.11) | copy-start | bytes 52
  13.5 9.3 %copy-start.4 = (bf16[2048,512]{1,0:T(8,128)(2,1)S(1)}, bf16[2048,512]{1,0:T(8,128)(2,1)}, u32[]{:S(2)}) copy-start(bf16[2048,512]{1,0:T(8,128)(2,1)} %param.15) | copy-start | bytes 6291460
  13.6 224.1 %all-to-all-start = ((bf16[256,4,2048]{0,2,1:T(8,128)(2,1)}), bf16[256,4,2048]{0,2,1:T(8,128)(2,1)}, u32[]{:S(2)}, u32[]{:S(2)}) async-start(bf16[256,4,2048]{0,2,1:T(8,128)(2,1)} %bitcast.75), calls=%async_computation | async-start | bytes 8388608 | tf_op jit(solution)/shard_map/all_to_all | solution.py:32
  20.2 5.2 %copy-start.8 = (bf16[2048]{0:T(1024)(128)(2,1)S(1)}, bf16[2048]{0:T(1024)(128)(2,1)}, u32[]{:S(2)}) copy-start(bf16[2048]{0:T(1024)(128)(2,1)} %param.14) | copy-start | bytes 12292
  20.2 209.5 %all-gather.4.cloned.1.call-start = ((), (), s32[]{:S(2)}) async-start(), calls=%async_computation.2 | async-start | bytes 2621440 | tf_op jit(solution)/shard_map/all_gather | solution.py:39
  21.5 4.1 %copy-start.3 = (bf16[512,512]{0,1:T(8,128)(2,1)S(1)}, bf16[512,512]{0,1:T(8,128)(2,1)}, u32[]{:S(2)}) copy-start(bf16[512,512]{0,1:T(8,128)(2,1)} %multiply_convert_fusion.7) | copy-start | bytes 1572868
  21.5 311.3 %all-reduce.2.cloned.1.call-start = ((), (), s32[]{:S(2)}) async-start(), calls=%async_computation.4 | async-start | bytes 4194304 | tf_op jit(solution)/shard_map/psum | solution.py:89
  237.6 6.4 %copy-start = (bf16[2048,512]{0,1:T(8,128)(2,1)S(1)}, bf16[2048,512]{0,1:T(8,128)(2,1)}, u32[]{:S(2)}) copy-start(bf16[2048,512]{0,1:T(8,128)(2,1)} %copy.36) | copy-start | bytes 6291460
  256.7 2.5 copy-start.2
  259.2 4.9 %copy-start.5 = (bf16[2048,512]{0,1:T(8,128)(2,1)S(1)}, bf16[2048,512]{0,1:T(8,128)(2,1)}, u32[]{:S(2)}) copy-start(bf16[2048,512]{0,1:T(8,128)(2,1)} %all-gather.4.cloned.1.call-done) | copy-start | bytes 6291460
  264.1 9.6 %copy-start.1 = (bf16[2048,512]{0,1:T(8,128)(2,1)S(1)}, bf16[2048,512]{0,1:T(8,128)(2,1)}, u32[]{:S(2)}) copy-start(bf16[2048,512]{0,1:T(8,128)(2,1)} %copy.36) | copy-start | bytes 6291460
  273.4 10.2 %copy-start.9 = (bf16[512]{0:T(512)(128)(2,1)S(1)}, bf16[512]{0:T(512)(128)(2,1)}, u32[]{:S(2)}) copy-start(bf16[512]{0:T(512)(128)(2,1)} %param.16) | copy-start | bytes 3076
  273.4 104.4 %reduce-scatter.2.cloned.1.call-start = ((), (), s32[]{:S(2)}) async-start(), calls=%async_computation.3 | async-start | bytes 2621440 | tf_op jit(solution)/shard_map/reduce_scatter | solution.py:84
Sparse Core Ops, SparseCore 0:
  23.1 77.2 all-gather.3
  273.6 59.1 all-reduce.1
  335.1 42.6 reduce-scatter.1
